TPU v7x, 32 devices: a whole 2x2x4 slice. The times are simulated.
32 devices in a mesh: seq: 8 (over z, y), head: 4 (over x, core).
Axes of the slice: x: 2, y: 2, z: 4, core: 2. Of those that a mesh axis runs over, the one named last changes fastest.
Arguments:
- queries: bfloat16 [8192, 512], P(('seq', 'head')), may hold values from -6 to 6
- key_rows: bfloat16 [8192, 128], P(('seq', 'head')), may hold values from -6 to 6
- value_rows: bfloat16 [8192, 128], P(('seq', 'head')), may hold values from -6 to 6
- out_grad: bfloat16 [8192, 512], P(('seq', 'head')), may hold values from -6 to 6
- doc_start: int32 [32], replicated, may hold values from 0 to 255
Outputs:
- outputs: bfloat16 [8192, 512], P(('seq', 'head'))
- query_grad: bfloat16 [8192, 512], P(('seq', 'head'))
- key_grad: bfloat16 [8192, 128], P(('seq', 'head'))
- value_grad: bfloat16 [8192, 128], P(('seq', 'head'))
Inputs may be any that keep to these rules, and one draw needn't show every extreme that they name: doc_start[c] is the position within span c of the first token of a new document.
All inputs are finite; a program needn't handle non-finite values.
Results may differ from a plain program's by a relative error of at most 0.0065.
Values may be sent and summed in bfloat16 or wider, within the bound.
No kernel may reach another device: no remote copies, remote signals or barrier semaphores. Data moves between devices by JAX's collectives and lax.ppermute only.
A program may use at most 128 MiB of HBM per device.

v0:
```python
import math

import jax
import jax.numpy as jnp
from jax import lax
from jax.experimental import pallas as pl
from jax.experimental.pallas import tpu as pltpu
from jax.sharding import PartitionSpec as P

HD = 128
GROUP = 4
SPANS_DEV = 4
SCALE = 1.0 / math.sqrt(HD)
LOG2_SCALE = SCALE * math.log2(math.e)
VMEM_GRANT = 16 * 1024 * 1024


masked_fill = -1e30


def passed_along(value, axis, steps):
    count = lax.axis_size(axis)
    first, last = (max(0, -steps), min(count, count - steps))
    return lax.ppermute(value, axis, [(source, source + steps) for source in range(first, last)])


def allowed_mask(
    first_row, row_count, key_count, halo_len, span_len, span_start, prev_begin, span_index
):
    row_pos = first_row + lax.broadcasted_iota(jnp.int32, (row_count, key_count), 0)
    col_pos = lax.broadcasted_iota(jnp.int32, (row_count, key_count), 1) - halo_len
    return (
        (col_pos <= row_pos)
        & ((col_pos >= span_start) | (span_start > row_pos))
        & (col_pos >= prev_begin - span_len)
        & ((col_pos >= 0) | (span_index > 0))
    )


def attend(query_rows, grad_rows, key_block, value_block, allowed, head_dim):
    score_scale = 1.0 / math.sqrt(head_dim)
    contract = (((2,), (2,)), ((0,), (0,)))
    forward = (((2,), (1,)), ((0,), (0,)))
    backward = (((1,), (1,)), ((0,), (0,)))
    scores = (
        lax.dot_general(query_rows, key_block, contract, preferred_element_type=jnp.float32)
        * score_scale
    )
    masked = jnp.where(allowed, scores, masked_fill)
    row_max = jnp.max(masked, axis=2, keepdims=True)
    exp_scores = jnp.where(allowed, jnp.exp(masked - row_max), 0.0)
    weights = exp_scores / jnp.sum(exp_scores, axis=2, keepdims=True)
    weights_low = weights.astype(jnp.bfloat16)
    result = lax.dot_general(
        weights_low, value_block, forward, preferred_element_type=jnp.float32
    ).astype(jnp.bfloat16)
    grad_weights = lax.dot_general(
        grad_rows, value_block, contract, preferred_element_type=jnp.float32
    )
    row_delta = jnp.sum(weights * grad_weights, axis=2, keepdims=True)
    grad_scores = (weights * (grad_weights - row_delta) * score_scale).astype(jnp.bfloat16)
    grad_query = lax.dot_general(
        grad_scores, key_block, forward, preferred_element_type=jnp.float32
    )
    grad_key = lax.dot_general(
        grad_scores, query_rows, backward, preferred_element_type=jnp.float32
    )
    grad_value = lax.dot_general(
        weights_low, grad_rows, backward, preferred_element_type=jnp.float32
    )
    return (result, grad_query, grad_key, grad_value)


def spans_over_devices(queries, key_rows, value_rows, out_grad, doc_start):
    tok_count = queries.shape[0]
    head_count = lax.axis_size("head")
    group_rows = tok_count * head_count
    span_len = group_rows // SPANS_DEV
    halo_len = span_len // 4
    half_len = span_len // 2
    rest_len = span_len - halo_len
    head_q, head_grad = (
        lax.all_to_all(queries, "head", split_axis=1, concat_axis=0, tiled=True),
        lax.all_to_all(out_grad, "head", split_axis=1, concat_axis=0, tiled=True),
    )
    full_k, full_v = (
        lax.all_gather(key_rows, "head", axis=0, tiled=True),
        lax.all_gather(value_rows, "head", axis=0, tiled=True),
    )
    column = lax.axis_index("head") // GROUP * HD
    head_k = lax.dynamic_slice_in_dim(full_k, column, HD, 1)
    head_v = lax.dynamic_slice_in_dim(full_v, column, HD, 1)
    query_3 = head_q.reshape(SPANS_DEV, span_len, HD)
    grad_3 = head_grad.reshape(SPANS_DEV, span_len, HD)
    keys_3 = head_k.reshape(SPANS_DEV, span_len, HD)
    values_3 = head_v.reshape(SPANS_DEV, span_len, HD)
    tail_k = keys_3[:, rest_len:]
    tail_v = values_3[:, rest_len:]
    edge_last_k, edge_last_v = passed_along(
        (tail_k[SPANS_DEV - 1], tail_v[SPANS_DEV - 1]), "seq", 1
    )
    edge_k = jnp.concatenate([edge_last_k[None], tail_k[: SPANS_DEV - 1]], axis=0)
    edge_v = jnp.concatenate([edge_last_v[None], tail_v[: SPANS_DEV - 1]], axis=0)
    key_block = jnp.concatenate([edge_k, keys_3], axis=1)
    value_block = jnp.concatenate([edge_v, values_3], axis=1)
    first_span = lax.axis_index("seq") * SPANS_DEV
    span_starts = lax.dynamic_slice_in_dim(doc_start, first_span, SPANS_DEV)
    before_start = lax.dynamic_slice_in_dim(doc_start, jnp.maximum(first_span - 1, 0), 1)
    prev_starts = jnp.concatenate([before_start, span_starts[: SPANS_DEV - 1]], axis=0)
    span_ids = first_span + jnp.arange(SPANS_DEV, dtype=jnp.int32)
    span_starts = span_starts.reshape(SPANS_DEV, 1, 1)
    prev_starts = prev_starts.reshape(SPANS_DEV, 1, 1)
    span_ids = span_ids.reshape(SPANS_DEV, 1, 1)
    grad_key = jnp.zeros((SPANS_DEV, halo_len + span_len, HD), jnp.float32)
    grad_value = jnp.zeros((SPANS_DEV, halo_len + span_len, HD), jnp.float32)
    results = []
    query_grads = []
    for block_index in range(2):
        first_row = block_index * half_len
        key_count = halo_len + first_row + half_len
        allowed = allowed_mask(
            first_row, half_len, key_count, halo_len, span_len, span_starts, prev_starts, span_ids
        )
        result, grad_query, part_key, part_value = attend(
            query_3[:, first_row : first_row + half_len],
            grad_3[:, first_row : first_row + half_len],
            key_block[:, :key_count],
            value_block[:, :key_count],
            allowed,
            HD,
        )
        results.append(result)
        query_grads.append(grad_query.astype(jnp.bfloat16))
        grad_key = grad_key.at[:, :key_count].add(part_key)
        grad_value = grad_value.at[:, :key_count].add(part_value)
    next_last_k, next_last_v = passed_along(
        (grad_key[0, :halo_len], grad_value[0, :halo_len]), "seq", -1
    )
    next_k = jnp.concatenate([grad_key[1:, :halo_len], next_last_k[None]], axis=0)
    next_v = jnp.concatenate([grad_value[1:, :halo_len], next_last_v[None]], axis=0)
    own_k = jnp.concatenate(
        [grad_key[:, halo_len : halo_len + rest_len], grad_key[:, halo_len + rest_len :] + next_k],
        axis=1,
    ).reshape(group_rows, HD)
    own_v = jnp.concatenate(
        [
            grad_value[:, halo_len : halo_len + rest_len],
            grad_value[:, halo_len + rest_len :] + next_v,
        ],
        axis=1,
    ).reshape(group_rows, HD)
    all_results = jnp.concatenate(results, axis=1).reshape(group_rows, HD)
    all_query_grads = jnp.concatenate(query_grads, axis=1).reshape(group_rows, HD)
    outputs, query_grad = (
        lax.all_to_all(all_results, "head", split_axis=0, concat_axis=1, tiled=True),
        lax.all_to_all(all_query_grads, "head", split_axis=0, concat_axis=1, tiled=True),
    )
    wide_gk, wide_gv = (
        lax.all_to_all(own_k, "head", split_axis=0, concat_axis=1, tiled=True),
        lax.all_to_all(own_v, "head", split_axis=0, concat_axis=1, tiled=True),
    )
    group_total = wide_gk.shape[1] // (GROUP * HD)
    key_grad = (
        wide_gk.reshape(tok_count, group_total, GROUP, HD)
        .sum(axis=2)
        .reshape(tok_count, group_total * HD)
        .astype(jnp.bfloat16)
    )
    value_grad = (
        wide_gv.reshape(tok_count, group_total, GROUP, HD)
        .sum(axis=2)
        .reshape(tok_count, group_total * HD)
        .astype(jnp.bfloat16)
    )
    return (outputs, query_grad, key_grad, value_grad)


ROWS_BY_ROWS = (((1,), (1,)), ((), ()))
COLS_BY_COLS = (((0,), (0,)), ((), ()))
PLAIN = (((1,), (0,)), ((), ()))


def dot(left, right, dims):
    return lax.dot_general(left, right, dims, preferred_element_type=jnp.float32)


def head_cols(head):
    return slice(head * HD, (head + 1) * HD)


def device_index():
    return lax.axis_index("seq") * lax.axis_size("head") + lax.axis_index("head")


def start_all(pairs, sems):
    copies = [pltpu.make_async_copy(source, target, sems.at[at]) for at, (source, target) in enumerate(pairs)]
    for copy in copies:
        copy.start()
    return copies


def side_by_side(ref, rows=slice(None)):
    return jnp.concatenate([ref[rows, head_cols(head)] for head in range(GROUP)], axis=0)


def sends_far(device):
    return (device % 2 == 1) & (device < device_count() - 1)


def write_info(span, doc_ref, info_ref):
    device = device_index()
    before = doc_ref[jnp.maximum(device - 1, 0)]
    row = lax.broadcasted_iota(jnp.int32, info_ref.shape, 0)
    first = jnp.where(device > 0, before - span, span)
    info_ref[...] = jnp.where(row == 0, doc_ref[device], first)


def pack_kernel(span, halo, doc_far, k_far, v_far, edge_ref, info_ref, doc_ref, sems):
    sends = sends_far(device_index())

    @pl.when(jnp.logical_not(sends))
    def _():
        edge_ref[...] = jnp.zeros_like(edge_ref)
        info_ref[...] = jnp.zeros_like(info_ref)

    @pl.when(sends)
    def _():
        tail = pl.ds(span - halo, halo)
        pairs = (
            (k_far.at[tail], edge_ref.at[:, :HD]),
            (v_far.at[tail], edge_ref.at[:, HD:]),
            (doc_far, doc_ref),
        )
        for copy in start_all(pairs, sems):
            copy.wait()
        write_info(span, doc_ref, info_ref)


def pair_pack_kernel(span, halo, k_ref, v_ref, edge_ref):
    edge_ref[:, :HD] = k_ref[span - halo :]
    edge_ref[:, HD:] = v_ref[span - halo :]


def own_kernel(
    span, halo, doc_far, far_info_ref, q_ref, g_ref, k_ref, v_ref,
    low_ref, high_ref, gw_low_ref, gw_high_ref, stat_ref, mask_ref, tail_ref, out_far, dq_far, dk_far, dv_far,
    doc_ref, info_ref, row_ref, out_ref, dq_ref, dk_ref, dv_ref, doc_sem, sems,
):
    half = span // 2
    device = device_index()

    @pl.when(sends_far(device))
    def _():
        info_ref[...] = far_info_ref[...]

    @pl.when(jnp.logical_not(sends_far(device)))
    def _():
        copy = pltpu.make_async_copy(doc_far, doc_ref, doc_sem)
        copy.start()
        copy.wait()
        write_info(span, doc_ref, info_ref)

    gw_low = dot(v_ref[:half], side_by_side(g_ref), ROWS_BY_ROWS)
    gw_high = dot(v_ref[half:], side_by_side(g_ref, slice(half, span)), ROWS_BY_ROWS)
    low = dot(k_ref[:half], side_by_side(q_ref), ROWS_BY_ROWS)
    high = dot(k_ref[half:], side_by_side(q_ref, slice(half, span)), ROWS_BY_ROWS)
    start = info_ref[0:1, :1]
    first = info_ref[1:2, :1]
    key_pos = lax.broadcasted_iota(jnp.int32, (half, span), 0)
    row_pos = lax.broadcasted_iota(jnp.int32, (half, span), 1)
    fill_low = jnp.where((key_pos <= row_pos) & ((key_pos >= start) | (start > row_pos)), 0.0, masked_fill)
    key_pos = half + lax.broadcasted_iota(jnp.int32, (half, half), 0)
    row_pos = half + lax.broadcasted_iota(jnp.int32, (half, half), 1)
    fill_high = jnp.where((key_pos <= row_pos) & ((key_pos >= start) | (start > row_pos)), 0.0, masked_fill)
    key_pos = lax.broadcasted_iota(jnp.int32, (halo, span), 0) - halo
    row_pos = lax.broadcasted_iota(jnp.int32, (halo, span), 1)
    halo_ok = ((key_pos >= start) | (start > row_pos)) & (key_pos >= first)
    mask_ref[...] = jnp.where(halo_ok, 0.0, masked_fill)
    for head in range(GROUP):
        wide = slice(head * span, (head + 1) * span)
        slim = slice(head * half, (head + 1) * half)
        part = low[:, wide] * LOG2_SCALE + fill_low
        part_high = high[:, slim] * LOG2_SCALE + fill_high
        top = jnp.max(part, axis=0, keepdims=True)
        top_high = jnp.maximum(top[:, half:], jnp.max(part_high, axis=0, keepdims=True))
        top = jnp.concatenate([top[:, :half], top_high], axis=1)
        part = jnp.exp2(part - top)
        part_high = jnp.exp2(part_high - top_high)
        total = jnp.sum(part, axis=0, keepdims=True)
        inner = jnp.sum(part * gw_low[:, wide], axis=0, keepdims=True)
        total_high = total[:, half:] + jnp.sum(part_high, axis=0, keepdims=True)
        inner_high = inner[:, half:] + jnp.sum(part_high * gw_high[:, slim], axis=0, keepdims=True)
        low_ref[:, wide] = part
        high_ref[:, slim] = part_high
        stat_ref[0:1, wide] = top
        stat_ref[1:2, wide] = jnp.concatenate([total[:, :half], total_high], axis=1)
        stat_ref[2:3, wide] = jnp.concatenate([inner[:, :half], inner_high], axis=1)
    gw_low_ref[...] = gw_low
    gw_high_ref[...] = gw_high

    @pl.when(device == 0)
    def _():
        share = 1.0 / stat_ref[1:2]
        row_ref[0:1] = share
        row_ref[1:2] = stat_ref[2:3] * share
        finish(
            span, halo, q_ref, g_ref, k_ref, v_ref, low_ref, high_ref, gw_low_ref, gw_high_ref, row_ref, None,
            (out_ref, dq_ref, dk_ref, dv_ref, tail_ref), (out_far, dq_far, dk_far, dv_far), sems,
        )


def halo_kernel(
    span, mask_ref, pair_ref, ring_ref, q_ref, g_ref, stat_ref, edge_ref, p_ref, ds_ref, row_ref, back_ref
):
    first = device_index() == 0

    @pl.when(first)
    def _():
        back_ref[...] = jnp.zeros_like(back_ref)

    @pl.when(jnp.logical_not(first))
    def _():
        queries = side_by_side(q_ref)
        grads = side_by_side(g_ref)
        mask = jnp.concatenate([mask_ref[...]] * GROUP, axis=1)
        device = device_index()
        edge = jnp.where((device % 2 == 1) | (device == ring_cut(1)), pair_ref[...], ring_ref[...])
        edge_ref[...] = edge
        scores = dot(edge[:, :HD], queries, ROWS_BY_ROWS) * LOG2_SCALE + mask
        grad_weights = dot(edge[:, HD:], grads, ROWS_BY_ROWS)
        own_top = stat_ref[0:1]
        top = jnp.maximum(jnp.max(scores, axis=0, keepdims=True), own_top)
        weights = jnp.exp2(scores - top)
        shift = jnp.exp2(own_top - top)
        total = stat_ref[1:2] * shift + jnp.sum(weights, axis=0, keepdims=True)
        inner = stat_ref[2:3] * shift + jnp.sum(weights * grad_weights, axis=0, keepdims=True)
        share = 1.0 / total
        delta = inner * share
        p = weights * share
        p_low = p.astype(jnp.bfloat16)
        ds_low = (p * (grad_weights - delta) * SCALE).astype(jnp.bfloat16)
        back_ref[:, :HD] = dot(ds_low, queries, PLAIN).astype(back_ref.dtype)
        back_ref[:, HD:] = dot(p_low, grads, PLAIN).astype(back_ref.dtype)
        p_ref[...] = p_low
        ds_ref[...] = ds_low
        row_ref[0:1] = shift * share
        row_ref[1:2] = delta


def finish(
    span, halo, q_ref, g_ref, k_ref, v_ref, low_ref, high_ref, gw_low_ref, gw_high_ref, row_ref, edge, near, far, sems
):
    out_ref, dq_ref, dk_ref, dv_ref, tail_ref = near
    half = span // 2
    nothing = jnp.zeros((half, half), jnp.bfloat16)
    share = row_ref[0:1]
    delta = row_ref[1:2]
    later = lambda row: jnp.concatenate(
        [row[:, head * span + half : (head + 1) * span] for head in range(GROUP)], axis=1
    )
    whole = lambda low, high: jnp.concatenate(
        [
            low,
            jnp.concatenate(
                [piece for head in range(GROUP) for piece in (nothing, high[:, head * half : (head + 1) * half])],
                axis=1,
            ),
        ],
        axis=0,
    )
    low = low_ref[...] * share
    high = high_ref[...] * later(share)
    p = whole(low.astype(jnp.bfloat16), high.astype(jnp.bfloat16))
    ds = whole(
        (low * (gw_low_ref[...] - delta) * SCALE).astype(jnp.bfloat16),
        (high * (gw_high_ref[...] - later(delta)) * SCALE).astype(jnp.bfloat16),
    )
    grad_key = dot(ds, side_by_side(q_ref), PLAIN)
    grad_value = dot(p, side_by_side(g_ref), PLAIN)
    keys = k_ref[...]
    values = v_ref[...]
    if edge is not None:
        edge_ref, p_ref, ds_ref = edge
        keys = jnp.concatenate([edge_ref[:, :HD], keys], axis=0)
        values = jnp.concatenate([edge_ref[:, HD:], values], axis=0)
        p = jnp.concatenate([p_ref[...], p], axis=0)
        ds = jnp.concatenate([ds_ref[...], ds], axis=0)
    out = dot(p, values, COLS_BY_COLS).astype(jnp.bfloat16)
    dq = dot(ds, keys, COLS_BY_COLS).astype(jnp.bfloat16)
    for head in range(GROUP):
        out_ref[:, head_cols(head)] = out[head * span : (head + 1) * span]
        dq_ref[:, head_cols(head)] = dq[head * span : (head + 1) * span]
    dk_ref[...] = grad_key.astype(jnp.bfloat16)
    dv_ref[...] = grad_value.astype(jnp.bfloat16)
    tail_ref[:, :HD] = grad_key[span - halo :]
    tail_ref[:, HD:] = grad_value[span - halo :]
    for copy in start_all(zip(near[:4], far), sems):
        copy.wait()


def rest_kernel(
    span, halo, q_ref, g_ref, k_ref, v_ref, edge_ref, low_ref, high_ref, gw_low_ref, gw_high_ref, p_ref, ds_ref,
    row_ref, out_in, dq_in, dk_in, dv_in, tail_in, out_far, dq_far, dk_far, dv_far, tail_ref,
    out_ref, dq_ref, dk_ref, dv_ref, sems,
):
    del out_in, dq_in, dk_in, dv_in, tail_in

    @pl.when(device_index() > 0)
    def _():
        finish(
            span, halo, q_ref, g_ref, k_ref, v_ref, low_ref, high_ref, gw_low_ref, gw_high_ref, row_ref,
            (edge_ref, p_ref, ds_ref), (out_ref, dq_ref, dk_ref, dv_ref, tail_ref),
            (out_far, dq_far, dk_far, dv_far), sems,
        )


def tail_kernel(span, halo, tail_ref, pair_ref, ring_ref, dk_in, dv_in, dk_far, dv_far, dk_ref, dv_ref, sems):
    del dk_in, dv_in
    device = device_index()
    back = jnp.where(device == ring_cut(-1) - 1, pair_ref[...], ring_ref[...]).astype(jnp.float32)
    total = tail_ref[...] + jnp.where(device == device_count() - 1, 0.0, back)
    dk_ref[...] = total[:, :HD].astype(jnp.bfloat16)
    dv_ref[...] = total[:, HD:].astype(jnp.bfloat16)
    last = pl.ds(span - halo, halo)
    for copy in start_all(((dk_ref, dk_far.at[last]), (dv_ref, dv_far.at[last])), sems):
        copy.wait()


def device_count():
    return lax.axis_size("seq") * lax.axis_size("head")


def ring_cut(steps):
    return device_count() // 4 - 2 if steps > 0 else device_count() // 2 - 2


def passed_on(value, pair_value, steps):
    count = device_count()
    cut = ring_cut(steps)
    rings = [(source, source + 1) for source in range(count)]
    rings[cut - 1] = (cut - 1, 0)
    rings[count - 1] = (count - 1, cut)
    pairs = [(source, source ^ 1) for source in range(count)]
    pairs[cut - 2 : cut + 2] = [(cut - 2, cut - 1), (cut - 1, cut), (cut, cut + 1), (cut + 1, cut - 2)]
    if steps < 0:
        rings, pairs = [[(target, source) for source, target in way] for way in (rings, pairs)]
    by_pair = lax.ppermute(pair_value, ("seq", "head"), pairs)
    return by_pair, lax.ppermute(value, ("seq", "head"), rings)


def span_on_device(queries, key_rows, value_rows, out_grad, doc_start):
    span = queries.shape[0]
    halo = span // 4
    wide, slim = (queries.shape, key_rows.shape)
    f32, bf16 = (jnp.float32, jnp.bfloat16)
    vmem = pl.BlockSpec(memory_space=pltpu.VMEM)
    hbm = pl.BlockSpec(memory_space=pltpu.HBM)
    near = lambda *values: [pltpu.with_memory_space_constraint(value, pltpu.VMEM) for value in values]
    far = lambda *values: [pltpu.with_memory_space_constraint(value, pltpu.HBM) for value in values]
    params = pltpu.CompilerParams(vmem_limit_bytes=VMEM_GRANT)
    results = [pltpu.VMEM(shape, bf16) for shape in (wide, wide, slim, slim)]
    results_far = [pltpu.HBM(shape, bf16) for shape in (wide, wide, slim, slim)]

    last_rows, info = pl.pallas_call(
        lambda *refs: pack_kernel(span, halo, *refs),
        in_specs=[hbm] * 3,
        out_specs=[vmem] * 2,
        out_shape=[pltpu.VMEM((halo, 2 * HD), bf16), pltpu.VMEM((8, HD), jnp.int32)],
        scratch_shapes=[pltpu.SMEM(doc_start.shape, jnp.int32), pltpu.SemaphoreType.DMA((3,))],
        compiler_params=params,
        cost_estimate=pl.CostEstimate(flops=4000000000, bytes_accessed=4 * 1024 * 1024, transcendentals=0),
        name="pack",
    )(*far(doc_start, key_rows, value_rows))
    pair_rows = pl.pallas_call(
        lambda *refs: pair_pack_kernel(span, halo, *refs),
        in_specs=[vmem] * 2,
        out_specs=vmem,
        out_shape=pltpu.VMEM((halo, 2 * HD), bf16),
        compiler_params=params,
        name="pair_pack",
    )(key_rows, value_rows)
    edges = passed_on(last_rows, pair_rows, 1)
    inputs = (queries, out_grad, key_rows, value_rows)
    low, high, gw_low, gw_high, stats, mask, tail, outputs, query_grad, key_grad, value_grad = pl.pallas_call(
        lambda *refs: own_kernel(span, halo, *refs),
        in_specs=[hbm] + [vmem] * 5,
        out_specs=[vmem] * 7 + [hbm] * 4,
        out_shape=[
            pltpu.VMEM((span // 2, GROUP * span), f32),
            pltpu.VMEM((span // 2, GROUP * span // 2), f32),
            pltpu.VMEM((span // 2, GROUP * span), f32),
            pltpu.VMEM((span // 2, GROUP * span // 2), f32),
            pltpu.VMEM((8, GROUP * span), f32),
            pltpu.VMEM((halo, span), f32),
            pltpu.VMEM((halo, 2 * HD), f32),
        ]
        + results_far,
        scratch_shapes=[
            pltpu.SMEM(doc_start.shape, jnp.int32),
            pltpu.VMEM((8, HD), jnp.int32),
            pltpu.VMEM((8, GROUP * span), f32),
        ]
        + results
        + [pltpu.SemaphoreType.DMA(()), pltpu.SemaphoreType.DMA((4,))],
        compiler_params=params,
        name="own_scores",
    )(*far(doc_start), *near(info), *inputs)
    edge, p_edge, ds_edge, rows, back = pl.pallas_call(
        lambda *refs: halo_kernel(span, *refs),
        in_specs=[vmem] * 6,
        out_specs=[vmem] * 5,
        out_shape=[
            pltpu.VMEM((halo, 2 * HD), bf16),
            pltpu.VMEM((halo, GROUP * span), bf16),
            pltpu.VMEM((halo, GROUP * span), bf16),
            pltpu.VMEM((8, GROUP * span), f32),
            pltpu.VMEM((halo, 2 * HD), bf16),
        ],
        compiler_params=params,
        name="halo_grads",
    )(*near(mask, *edges), *inputs[:2], *near(stats))
    returned = passed_on(back, back, -1)
    outputs, query_grad, key_grad, value_grad, tail = pl.pallas_call(
        lambda *refs: rest_kernel(span, halo, *refs),
        in_specs=[vmem] * 12 + [hbm] * 4 + [vmem],
        out_specs=[hbm] * 4 + [vmem],
        out_shape=results_far + [pltpu.VMEM((halo, 2 * HD), f32)],
        scratch_shapes=results + [pltpu.SemaphoreType.DMA((4,))],
        input_output_aliases={12: 0, 13: 1, 14: 2, 15: 3, 16: 4},
        compiler_params=params,
        name="own_grads",
    )(
        *inputs,
        *near(edge, low, high, gw_low, gw_high, p_edge, ds_edge, rows),
        *far(outputs, query_grad, key_grad, value_grad),
        *near(tail),
    )
    key_grad, value_grad = pl.pallas_call(
        lambda *refs: tail_kernel(span, halo, *refs),
        in_specs=[vmem, vmem, vmem, hbm, hbm],
        out_specs=[hbm, hbm],
        out_shape=results_far[2:],
        scratch_shapes=[pltpu.VMEM((halo, HD), bf16)] * 2 + [pltpu.SemaphoreType.DMA((2,))],
        input_output_aliases={3: 0, 4: 1},
        compiler_params=params,
        name="tail_grads",
    )(*near(tail, *returned), *far(key_grad, value_grad))
    return (outputs, query_grad, key_grad, value_grad)


def per_device(queries, key_rows, value_rows, out_grad, doc_start):
    span = queries.shape[0] * lax.axis_size("head") // SPANS_DEV
    whole_span = span == queries.shape[0] and key_rows.shape[1] == HD and queries.shape[1] == GROUP * HD
    whole_span = whole_span and device_count() % 8 == 0 and device_count() >= 16
    plan = span_on_device if whole_span else spans_over_devices
    return plan(queries, key_rows, value_rows, out_grad, doc_start)


def solution(mesh):
    placed = (
        P(("seq", "head"), None),
        P(("seq", "head"), None),
        P(("seq", "head"), None),
        P(("seq", "head"), None),
        P(),
    )
    return jax.shard_map(
        per_device,
        mesh=mesh,
        in_specs=placed,
        out_specs=(
            P(("seq", "head"), None),
            P(("seq", "head"), None),
            P(("seq", "head"), None),
            P(("seq", "head"), None),
        ),
        check_vma=False,
    )
```

profile of v0, /device:TPU:7, one launch (start us, length us, event | category | flops | bytes accessed | tf_op | source)
XLA Modules:
  0.0 10.5 jit_solution(14518957714222431775)
XLA Ops:
  0.6 0.0 copy-start.3
  0.6 0.0 copy-start.2
  0.7 0.0 copy-start
  0.7 0.0 copy-start.1
  0.7 0.9 %pack.1 = (bf16[64,256]{1,0:T(8,128)(2,1)S(1)}, s32[8,128]{1,0:T(8,128)S(1)}) custom-call(s32[32]{0:T(128)} %refs_0_.5, bf16[256,128]{1,0:T(8,128)(2,1)} %refs_2_.5, bf16[256,128]{1,0:T(8,128)(2,1)} %refs_3_.5), custom_call_target="tpu_custom_call" | custom-call | flops 4000000000 | bytes 4194304 | tf_op jit(solution)/shard_map/pack/pallas_call | solution.py:464
  1.5 1.0 %collective-permute-start.1 = (bf16[64,256]{1,0:T(8,128)(2,1)S(1)}, bf16[64,256]{1,0:T(8,128)(2,1)S(1)}, u32[]{:S(2)}, u32[]{:S(2)}) collective-permute-start(bf16[64,256]{1,0:T(8,128)(2,1)S(1)} %get-tuple-element.31), channel_id=1, source_target_pairs={{0,1},{1,2},{2,3},{3,4},{4,5},{5,0},{6,7},{7,8},{8,9},{9,10},{10,1... | collective-permute-start | bytes 98312 | tf_op jit(solution)/shard_map/ppermute | solution.py:448
  2.6 0.0 copy-done.3
  2.6 0.0 copy-done.2
  2.6 0.1 collective-permute-start
  2.7 0.0 copy-done
  2.7 0.0 copy-done.1
  2.7 0.7 %own_scores.1 = (f32[128,1024]{1,0:T(8,128)S(1)}, f32[128,512]{1,0:T(8,128)S(1)}, f32[128,1024]{1,0:T(8,128)S(1)}, f32[128,512]{1,0:T(8,128)S(1)}, f32[8,1024]{1...) custom-call(s32[32]{0:T(128)} %refs_0_.5, ...), custom_call_target="tpu_custom_call" | custom-call | tf_op jit(solution)/shard_map/own_scores/pallas_call | solution.py:484
  3.4 0.2 %collective-permute-done.1.refs_2_ = bf16[64,256]{1,0:T(8,128)(2,1)S(1)} collective-permute-done((bf16[64,256]{1,0:T(8,128)(2,1)S(1)}, bf16[64,256]{1,0:T(8,128)(2,1)S(1)}, u32[]{:S(2)}, u32[]{:S(2)}) %collective-permute-start.1) | collective-permute-done | bytes 32800 | tf_op jit(solution)/shard_map/ppermute | solution.py:448
  3.6 0.3 %collective-permute-done.refs_1_ = bf16[64,256]{1,0:T(8,128)(2,1)S(1)} collective-permute-done((bf16[64,256]{1,0:T(8,128)(2,1)S(1)}, bf16[64,256]{1,0:T(8,128)(2,1)S(1)}, u32[]{:S(2)}, u32[]{:S(2)}) %collective-permute-start) | collective-permute-done | bytes 32800 | tf_op jit(solution)/shard_map/ppermute | solution.py:447
  3.9 0.5 %halo_grads.1 = (bf16[64,256]{1,0:T(8,128)(2,1)S(1)}, bf16[64,1024]{1,0:T(8,128)(2,1)S(1)}, bf16[64,1024]{1,0:T(8,128)(2,1)S(1)}, f32[8,1024]{1,0:T(8,128)S(1)}, bf16[64,256]{1,0:T(8,128)(2,1)S(1)}) custom-call(f32[64,256]{1,0:T(8,128)S(1)} %get-tuple-element.30.refs_0_, bf16[64,256]{1,0:T(8,128)(2,1)S(1)} %collective-permute-done.refs_1_, ...), custom_call_target="tpu_custom_call" | custom-call | tf_op jit(solution)/shard_map/halo_grads/pallas_call | solution.py:508
  4.4 2.8 %collective-permute-start.3 = (bf16[64,256]{1,0:T(8,128)(2,1)S(1)}, bf16[64,256]{1,0:T(8,128)(2,1)S(1)}, u32[]{:S(2)}, u32[]{:S(2)}) collective-permute-start(bf16[64,256]{1,0:T(8,128)(2,1)S(1)} %get-tuple-element.49), channel_id=1, source_target_pairs={{1,0},{2,1},{3,2},{4,3},{5,4},{6,5},{7,6},{8,7},{9,8},{10,9},{11,1... | collective-permute-start | bytes 98312 | tf_op jit(solution)/shard_map/ppermute | solution.py:448
  7.2 0.1 collective-permute-start.2
  7.3 1.6 %own_grads.1 = (bf16[256,512]{1,0:T(8,128)(2,1)}, bf16[256,512]{1,0:T(8,128)(2,1)}, bf16[256,128]{1,0:T(8,128)(2,1)}, bf16[256,128]{1,0:T(8,128)(2,1)}, f32[64,256]{1,0:T(8,128)S(1)}) custom-call(bf16[256,512]{1,0:T(8,128)(2,1)S(1)} %copy-done, ...), custom_call_target="tpu_custom_call", output_to_operand_aliasing={{0}: (12, {}), {1}: (13, {}), {2}: (14, {}), {3}: (15, {}),... | custom-call | tf_op jit(solution)/shard_map/own_grads/pallas_call | solution.py:523
  8.9 1.0 %collective-permute-done.3.refs_2_ = bf16[64,256]{1,0:T(8,128)(2,1)S(1)} collective-permute-done((bf16[64,256]{1,0:T(8,128)(2,1)S(1)}, bf16[64,256]{1,0:T(8,128)(2,1)S(1)}, u32[]{:S(2)}, u32[]{:S(2)}) %collective-permute-start.3) | collective-permute-done | bytes 32800 | tf_op jit(solution)/shard_map/ppermute | solution.py:448
  9.9 0.0 collective-permute-done.2.refs_1_
  9.9 0.6 %tail_grads.1 = (bf16[256,128]{1,0:T(8,128)(2,1)}, bf16[256,128]{1,0:T(8,128)(2,1)}) custom-call(f32[64,256]{1,0:T(8,128)S(1)} %get-tuple-element.48.refs_0_, bf16[64,256]{1,0:T(8,128)(2,1)S(1)} %collective-permute-done.2.refs_1_, bf16[64,256]{1,0:T(8,128)(2,1)S(1)} %collective-permute-done.3.refs_2_, ...), custom_call_target="tpu_custom_call", output_to_operand_aliasing={{0}: (3, {}), {1}: (4, {})} | custom-call | tf_op jit(solution)/shard_map/tail_grads/pallas_call | solution.py:538
  (1 shorter events, 0.0 us)
Async XLA Ops:
  0.6 1.9 %copy-start.3 = (bf16[256,128]{1,0:T(8,128)(2,1)S(1)}, bf16[256,128]{1,0:T(8,128)(2,1)}, u32[]{:S(2)}) copy-start(bf16[256,128]{1,0:T(8,128)(2,1)} %refs_3_.5) | copy-start | bytes 196612
  0.6 1.9 %copy-start.2 = (bf16[256,128]{1,0:T(8,128)(2,1)S(1)}, bf16[256,128]{1,0:T(8,128)(2,1)}, u32[]{:S(2)}) copy-start(bf16[256,128]{1,0:T(8,128)(2,1)} %refs_2_.5) | copy-start | bytes 196612
  0.7 2.0 %copy-start = (bf16[256,512]{1,0:T(8,128)(2,1)S(1)}, bf16[256,512]{1,0:T(8,128)(2,1)}, u32[]{:S(2)}) copy-start(bf16[256,512]{1,0:T(8,128)(2,1)} %refs_0_.7) | copy-start | bytes 786436
  0.7 2.0 %copy-start.1 = (bf16[256,512]{1,0:T(8,128)(2,1)S(1)}, bf16[256,512]{1,0:T(8,128)(2,1)}, u32[]{:S(2)}) copy-start(bf16[256,512]{1,0:T(8,128)(2,1)} %refs_1_.5) | copy-start | bytes 786436
  1.5 2.0 %collective-permute-start.1 = (bf16[64,256]{1,0:T(8,128)(2,1)S(1)}, bf16[64,256]{1,0:T(8,128)(2,1)S(1)}, u32[]{:S(2)}, u32[]{:S(2)}) collective-permute-start(bf16[64,256]{1,0:T(8,128)(2,1)S(1)} %get-tuple-element.31), channel_id=1, source_target_pairs={{0,1},{1,2},{2,3},{3,4},{4,5},{5,0},{6,7},{7,8},{8,9},{9,10},{10,1... | collective-permute-start | bytes 98312 | tf_op jit(solution)/shard_map/ppermute | solution.py:448
  2.6 1.3 %collective-permute-start = (bf16[64,256]{1,0:T(8,128)(2,1)S(1)}, bf16[64,256]{1,0:T(8,128)(2,1)S(1)}, u32[]{:S(2)}, u32[]{:S(2)}) collective-permute-start(bf16[64,256]{1,0:T(8,128)(2,1)S(1)} %pair_pack.1), channel_id=1, source_target_pairs={{0,1},{1,0},{2,3},{3,2},{4,5},{5,6},{6,7},{7,4},{8,9},{9,8},{10,11... | collective-permute-start | bytes 98312 | tf_op jit(solution)/shard_map/ppermute | solution.py:447
  4.4 5.5 %collective-permute-start.3 = (bf16[64,256]{1,0:T(8,128)(2,1)S(1)}, bf16[64,256]{1,0:T(8,128)(2,1)S(1)}, u32[]{:S(2)}, u32[]{:S(2)}) collective-permute-start(bf16[64,256]{1,0:T(8,128)(2,1)S(1)} %get-tuple-element.49), channel_id=1, source_target_pairs={{1,0},{2,1},{3,2},{4,3},{5,4},{6,5},{7,6},{8,7},{9,8},{10,9},{11,1... | collective-permute-start | bytes 98312 | tf_op jit(solution)/shard_map/ppermute | solution.py:448
  7.2 2.7 %collective-permute-start.2 = (bf16[64,256]{1,0:T(8,128)(2,1)S(1)}, bf16[64,256]{1,0:T(8,128)(2,1)S(1)}, u32[]{:S(2)}, u32[]{:S(2)}) collective-permute-start(bf16[64,256]{1,0:T(8,128)(2,1)S(1)} %get-tuple-element.49), channel_id=1, source_target_pairs={{1,0},{0,1},{3,2},{2,3},{5,4},{4,5},{7,6},{6,7},{9,8},{8,9},{11,10... | collective-permute-start | bytes 98312 | tf_op jit(solution)/shard_map/ppermute | solution.py:447
where the time goes:
time: 10.7 us; the launch traced here: 10.5 us
  Pallas kernels  4.36 us (41%)
  starting transfers between devices  3.98 us (37%)
  waiting for transfers between devices  1.46 us (14%)
  between operations  0.73 us (7%)
    ppermute x2, starting transfers between devices, passed_on(): return (by_pair, lax.ppermute(value, ('seq', 'head'), rings))  3.82 us
    pallas_call x1, Pallas kernels, span_on_device(): pl.pallas_call(lambda *refs: rest_kernel(span, halo, *refs), in_specs=[vm...  1.63 us
    ppermute x2, waiting for transfers between devices, passed_on(): return (by_pair, lax.ppermute(value, ('seq', 'head'), rings))  1.18 us
    pallas_call x1, Pallas kernels, span_on_device(): pl.pallas_call(lambda *refs: pack_kernel(span, halo, *refs), in_specs=[hb...  0.86 us
    pallas_call x1, Pallas kernels, span_on_device(): pl.pallas_call(lambda *refs: own_kernel(span, halo, *refs), in_specs=[hbm...  0.68 us
    pallas_call x1, Pallas kernels, span_on_device(): pl.pallas_call(lambda *refs: tail_kernel(span, halo, *refs), in_specs=[vm...  0.64 us
    pallas_call x1, Pallas kernels, span_on_device(): pl.pallas_call(lambda *refs: halo_kernel(span, *refs), in_specs=[vmem] *...  0.54 us
    ppermute x2, waiting for transfers between devices, passed_on(): by_pair = lax.ppermute(pair_value, ('seq', 'head'), pairs)  0.27 us
  transfers between devices with their start and end apart: 4, of which 3 were waited for; matrix products, arithmetic and copies ran while one was open for 0% of the time, Pallas kernels for 22%

commit v1 on v0

--- a/solution.py
+++ b/solution.py
@@ -312,39 +312,31 @@
 def halo_kernel(
     span, mask_ref, pair_ref, ring_ref, q_ref, g_ref, stat_ref, edge_ref, p_ref, ds_ref, row_ref, back_ref
 ):
-    first = device_index() == 0
-
-    @pl.when(first)
-    def _():
-        back_ref[...] = jnp.zeros_like(back_ref)
-
-    @pl.when(jnp.logical_not(first))
-    def _():
-        queries = side_by_side(q_ref)
-        grads = side_by_side(g_ref)
-        mask = jnp.concatenate([mask_ref[...]] * GROUP, axis=1)
-        device = device_index()
-        edge = jnp.where((device % 2 == 1) | (device == ring_cut(1)), pair_ref[...], ring_ref[...])
-        edge_ref[...] = edge
-        scores = dot(edge[:, :HD], queries, ROWS_BY_ROWS) * LOG2_SCALE + mask
-        grad_weights = dot(edge[:, HD:], grads, ROWS_BY_ROWS)
-        own_top = stat_ref[0:1]
-        top = jnp.maximum(jnp.max(scores, axis=0, keepdims=True), own_top)
-        weights = jnp.exp2(scores - top)
-        shift = jnp.exp2(own_top - top)
-        total = stat_ref[1:2] * shift + jnp.sum(weights, axis=0, keepdims=True)
-        inner = stat_ref[2:3] * shift + jnp.sum(weights * grad_weights, axis=0, keepdims=True)
-        share = 1.0 / total
-        delta = inner * share
-        p = weights * share
-        p_low = p.astype(jnp.bfloat16)
-        ds_low = (p * (grad_weights - delta) * SCALE).astype(jnp.bfloat16)
-        back_ref[:, :HD] = dot(ds_low, queries, PLAIN).astype(back_ref.dtype)
-        back_ref[:, HD:] = dot(p_low, grads, PLAIN).astype(back_ref.dtype)
-        p_ref[...] = p_low
-        ds_ref[...] = ds_low
-        row_ref[0:1] = shift * share
-        row_ref[1:2] = delta
+    queries = side_by_side(q_ref)
+    grads = side_by_side(g_ref)
+    mask = jnp.concatenate([mask_ref[...]] * GROUP, axis=1)
+    device = device_index()
+    edge = jnp.where((device % 2 == 1) | (device == ring_cut(1)), pair_ref[...], ring_ref[...])
+    edge_ref[...] = edge
+    scores = dot(edge[:, :HD], queries, ROWS_BY_ROWS) * LOG2_SCALE + mask
+    grad_weights = dot(edge[:, HD:], grads, ROWS_BY_ROWS)
+    own_top = stat_ref[0:1]
+    top = jnp.maximum(jnp.max(scores, axis=0, keepdims=True), own_top)
+    weights = jnp.exp2(scores - top)
+    shift = jnp.exp2(own_top - top)
+    total = stat_ref[1:2] * shift + jnp.sum(weights, axis=0, keepdims=True)
+    inner = stat_ref[2:3] * shift + jnp.sum(weights * grad_weights, axis=0, keepdims=True)
+    share = 1.0 / total
+    delta = inner * share
+    p = weights * share
+    p_low = p.astype(jnp.bfloat16)
+    ds_low = (p * (grad_weights - delta) * SCALE).astype(jnp.bfloat16)
+    back_ref[:, :HD] = dot(ds_low, queries, PLAIN).astype(back_ref.dtype)
+    back_ref[:, HD:] = dot(p_low, grads, PLAIN).astype(back_ref.dtype)
+    p_ref[...] = p_low
+    ds_ref[...] = ds_low
+    row_ref[0:1] = shift * share
+    row_ref[1:2] = delta
 
 
 def finish(
@@ -431,7 +423,7 @@
 
 
 def ring_cut(steps):
-    return device_count() // 4 - 2 if steps > 0 else device_count() // 2 - 2
+    return device_count() // 2 + (2 if steps > 0 else -2)
 
 
 def passed_on(value, pair_value, steps):

time: 10.7 us -> 10.7 us (level)
  starting transfers between devices: 3.98 us -> 2.18 us
  waiting for transfers between devices: 1.46 us -> 3.26 us
    ppermute x2, waiting for transfers between devices: 1.18 us -> 3.02 us  [passed_on(): return (by_pair, lax.ppermute(value, ('seq', 'head'), rings))]
    ppermute x2, starting transfers between devices: 3.82 us -> 2.06 us  [passed_on(): return (by_pair, lax.ppermute(value, ('seq', 'head'), rings))]
where the time goes in v1:
time: 10.7 us; the launch traced here: 10.5 us
  Pallas kernels  4.36 us (41%)
  waiting for transfers between devices  3.26 us (30%)
  starting transfers between devices  2.18 us (20%)
  between operations  0.73 us (7%)
    ppermute x2, waiting for transfers between devices, passed_on(): return (by_pair, lax.ppermute(value, ('seq', 'head'), rings))  3.02 us
    ppermute x2, starting transfers between devices, passed_on(): return (by_pair, lax.ppermute(value, ('seq', 'head'), rings))  2.06 us
    pallas_call x1, Pallas kernels, span_on_device(): pl.pallas_call(lambda *refs: rest_kernel(span, halo, *refs), in_specs=[vm...  1.63 us
    pallas_call x1, Pallas kernels, span_on_device(): pl.pallas_call(lambda *refs: pack_kernel(span, halo, *refs), in_specs=[hb...  0.86 us
    pallas_call x1, Pallas kernels, span_on_device(): pl.pallas_call(lambda *refs: own_kernel(span, halo, *refs), in_specs=[hbm...  0.68 us
    pallas_call x1, Pallas kernels, span_on_device(): pl.pallas_call(lambda *refs: tail_kernel(span, halo, *refs), in_specs=[vm...  0.64 us
    pallas_call x1, Pallas kernels, span_on_device(): pl.pallas_call(lambda *refs: halo_kernel(span, *refs), in_specs=[vmem] *...  0.54 us
    ppermute x2, waiting for transfers between devices, passed_on(): by_pair = lax.ppermute(pair_value, ('seq', 'head'), pairs)  0.24 us
  transfers between devices with their start and end apart: 4, of which 3 were waited for; matrix products, arithmetic and copies ran while one was open for 0% of the time, Pallas kernels for 22%

profile of v1, /device:TPU:7, one launch (start us, length us, event | category | flops | bytes accessed | tf_op | source)
XLA Modules:
  0.0 10.5 jit_solution(5576438219957952695)
XLA Ops:
  0.6 0.0 copy-start.3
  0.6 0.0 copy-start.2
  0.7 0.0 copy-start
  0.7 0.0 copy-start.1
  0.7 0.9 %pack.1 = (bf16[64,256]{1,0:T(8,128)(2,1)S(1)}, s32[8,128]{1,0:T(8,128)S(1)}) custom-call(s32[32]{0:T(128)} %refs_0_.5, bf16[256,128]{1,0:T(8,128)(2,1)} %refs_2_.5, bf16[256,128]{1,0:T(8,128)(2,1)} %refs_3_.5), custom_call_target="tpu_custom_call" | custom-call | flops 4000000000 | bytes 4194304 | tf_op jit(solution)/shard_map/pack/pallas_call | solution.py:456
  1.5 1.0 %collective-permute-start.1 = (bf16[64,256]{1,0:T(8,128)(2,1)S(1)}, bf16[64,256]{1,0:T(8,128)(2,1)S(1)}, u32[]{:S(2)}, u32[]{:S(2)}) collective-permute-start(bf16[64,256]{1,0:T(8,128)(2,1)S(1)} %get-tuple-element.31), channel_id=1, source_target_pairs={{0,1},{1,2},{2,3},{3,4},{4,5},{5,6},{6,7},{7,8},{8,9},{9,10},{10,1... | collective-permute-start | bytes 98312 | tf_op jit(solution)/shard_map/ppermute | solution.py:440
  2.6 0.0 copy-done.3
  2.6 0.0 copy-done.2
  2.6 0.0 collective-permute-start
  2.6 0.0 copy-done
  2.6 0.0 copy-done.1
  2.6 0.7 %own_scores.1 = (f32[128,1024]{1,0:T(8,128)S(1)}, f32[128,512]{1,0:T(8,128)S(1)}, f32[128,1024]{1,0:T(8,128)S(1)}, f32[128,512]{1,0:T(8,128)S(1)}, f32[8,1024]{1...) custom-call(s32[32]{0:T(128)} %refs_0_.5, ...), custom_call_target="tpu_custom_call" | custom-call | tf_op jit(solution)/shard_map/own_scores/pallas_call | solution.py:476
  3.3 0.3 %collective-permute-done.1.refs_2_ = bf16[64,256]{1,0:T(8,128)(2,1)S(1)} collective-permute-done((bf16[64,256]{1,0:T(8,128)(2,1)S(1)}, bf16[64,256]{1,0:T(8,128)(2,1)S(1)}, u32[]{:S(2)}, u32[]{:S(2)}) %collective-permute-start.1) | collective-permute-done | bytes 32800 | tf_op jit(solution)/shard_map/ppermute | solution.py:440
  3.6 0.2 %collective-permute-done.refs_1_ = bf16[64,256]{1,0:T(8,128)(2,1)S(1)} collective-permute-done((bf16[64,256]{1,0:T(8,128)(2,1)S(1)}, bf16[64,256]{1,0:T(8,128)(2,1)S(1)}, u32[]{:S(2)}, u32[]{:S(2)}) %collective-permute-start) | collective-permute-done | bytes 32800 | tf_op jit(solution)/shard_map/ppermute | solution.py:439
  3.8 0.5 %halo_grads.1 = (bf16[64,256]{1,0:T(8,128)(2,1)S(1)}, bf16[64,1024]{1,0:T(8,128)(2,1)S(1)}, bf16[64,1024]{1,0:T(8,128)(2,1)S(1)}, f32[8,1024]{1,0:T(8,128)S(1)}, bf16[64,256]{1,0:T(8,128)(2,1)S(1)}) custom-call(f32[64,256]{1,0:T(8,128)S(1)} %get-tuple-element.30.refs_0_, bf16[64,256]{1,0:T(8,128)(2,1)S(1)} %collective-permute-done.refs_1_, ...), custom_call_target="tpu_custom_call" | custom-call | tf_op jit(solution)/shard_map/halo_grads/pallas_call | solution.py:500
  4.4 1.0 %collective-permute-start.3 = (bf16[64,256]{1,0:T(8,128)(2,1)S(1)}, bf16[64,256]{1,0:T(8,128)(2,1)S(1)}, u32[]{:S(2)}, u32[]{:S(2)}) collective-permute-start(bf16[64,256]{1,0:T(8,128)(2,1)S(1)} %get-tuple-element.49), channel_id=1, source_target_pairs={{1,0},{2,1},{3,2},{4,3},{5,4},{6,5},{7,6},{8,7},{9,8},{10,9},{11,1... | collective-permute-start | bytes 98312 | tf_op jit(solution)/shard_map/ppermute | solution.py:440
  5.4 0.1 collective-permute-start.2
  5.5 1.6 %own_grads.1 = (bf16[256,512]{1,0:T(8,128)(2,1)}, bf16[256,512]{1,0:T(8,128)(2,1)}, bf16[256,128]{1,0:T(8,128)(2,1)}, bf16[256,128]{1,0:T(8,128)(2,1)}, f32[64,256]{1,0:T(8,128)S(1)}) custom-call(bf16[256,512]{1,0:T(8,128)(2,1)S(1)} %copy-done, ...), custom_call_target="tpu_custom_call", output_to_operand_aliasing={{0}: (12, {}), {1}: (13, {}), {2}: (14, {}), {3}: (15, {}),... | custom-call | tf_op jit(solution)/shard_map/own_grads/pallas_call | solution.py:515
  7.1 2.8 %collective-permute-done.3.refs_2_ = bf16[64,256]{1,0:T(8,128)(2,1)S(1)} collective-permute-done((bf16[64,256]{1,0:T(8,128)(2,1)S(1)}, bf16[64,256]{1,0:T(8,128)(2,1)S(1)}, u32[]{:S(2)}, u32[]{:S(2)}) %collective-permute-start.3) | collective-permute-done | bytes 32800 | tf_op jit(solution)/shard_map/ppermute | solution.py:440
  9.9 0.0 collective-permute-done.2.refs_1_
  9.9 0.6 %tail_grads.1 = (bf16[256,128]{1,0:T(8,128)(2,1)}, bf16[256,128]{1,0:T(8,128)(2,1)}) custom-call(f32[64,256]{1,0:T(8,128)S(1)} %get-tuple-element.48.refs_0_, bf16[64,256]{1,0:T(8,128)(2,1)S(1)} %collective-permute-done.2.refs_1_, bf16[64,256]{1,0:T(8,128)(2,1)S(1)} %collective-permute-done.3.refs_2_, ...), custom_call_target="tpu_custom_call", output_to_operand_aliasing={{0}: (3, {}), {1}: (4, {})} | custom-call | tf_op jit(solution)/shard_map/tail_grads/pallas_call | solution.py:530
  (1 shorter events, 0.0 us)
Async XLA Ops:
  0.6 1.9 %copy-start.3 = (bf16[256,128]{1,0:T(8,128)(2,1)S(1)}, bf16[256,128]{1,0:T(8,128)(2,1)}, u32[]{:S(2)}) copy-start(bf16[256,128]{1,0:T(8,128)(2,1)} %refs_3_.5) | copy-start | bytes 196612
  0.6 1.9 %copy-start.2 = (bf16[256,128]{1,0:T(8,128)(2,1)S(1)}, bf16[256,128]{1,0:T(8,128)(2,1)}, u32[]{:S(2)}) copy-start(bf16[256,128]{1,0:T(8,128)(2,1)} %refs_2_.5) | copy-start | bytes 196612
  0.7 2.0 %copy-start = (bf16[256,512]{1,0:T(8,128)(2,1)S(1)}, bf16[256,512]{1,0:T(8,128)(2,1)}, u32[]{:S(2)}) copy-start(bf16[256,512]{1,0:T(8,128)(2,1)} %refs_0_.7) | copy-start | bytes 786436
  0.7 2.0 %copy-start.1 = (bf16[256,512]{1,0:T(8,128)(2,1)S(1)}, bf16[256,512]{1,0:T(8,128)(2,1)}, u32[]{:S(2)}) copy-start(bf16[256,512]{1,0:T(8,128)(2,1)} %refs_1_.5) | copy-start | bytes 786436
  1.5 2.0 %collective-permute-start.1 = (bf16[64,256]{1,0:T(8,128)(2,1)S(1)}, bf16[64,256]{1,0:T(8,128)(2,1)S(1)}, u32[]{:S(2)}, u32[]{:S(2)}) collective-permute-start(bf16[64,256]{1,0:T(8,128)(2,1)S(1)} %get-tuple-element.31), channel_id=1, source_target_pairs={{0,1},{1,2},{2,3},{3,4},{4,5},{5,6},{6,7},{7,8},{8,9},{9,10},{10,1... | collective-permute-start | bytes 98312 | tf_op jit(solution)/shard_map/ppermute | solution.py:440
  2.6 1.2 %collective-permute-start = (bf16[64,256]{1,0:T(8,128)(2,1)S(1)}, bf16[64,256]{1,0:T(8,128)(2,1)S(1)}, u32[]{:S(2)}, u32[]{:S(2)}) collective-permute-start(bf16[64,256]{1,0:T(8,128)(2,1)S(1)} %pair_pack.1), channel_id=1, source_target_pairs={{0,1},{1,0},{2,3},{3,2},{4,5},{5,4},{6,7},{7,6},{8,9},{9,8},{10,11... | collective-permute-start | bytes 98312 | tf_op jit(solution)/shard_map/ppermute | solution.py:439
  4.4 5.5 %collective-permute-start.3 = (bf16[64,256]{1,0:T(8,128)(2,1)S(1)}, bf16[64,256]{1,0:T(8,128)(2,1)S(1)}, u32[]{:S(2)}, u32[]{:S(2)}) collective-permute-start(bf16[64,256]{1,0:T(8,128)(2,1)S(1)} %get-tuple-element.49), channel_id=1, source_target_pairs={{1,0},{2,1},{3,2},{4,3},{5,4},{6,5},{7,6},{8,7},{9,8},{10,9},{11,1... | collective-permute-start | bytes 98312 | tf_op jit(solution)/shard_map/ppermute | solution.py:440
  5.4 4.5 %collective-permute-start.2 = (bf16[64,256]{1,0:T(8,128)(2,1)S(1)}, bf16[64,256]{1,0:T(8,128)(2,1)S(1)}, u32[]{:S(2)}, u32[]{:S(2)}) collective-permute-start(bf16[64,256]{1,0:T(8,128)(2,1)S(1)} %get-tuple-element.49), channel_id=1, source_target_pairs={{1,0},{0,1},{3,2},{2,3},{5,4},{4,5},{7,6},{6,7},{9,8},{8,9},{11,10... | collective-permute-start | bytes 98312 | tf_op jit(solution)/shard_map/ppermute | solution.py:439

commit v2 on v1

--- a/solution.py
+++ b/solution.py
@@ -243,7 +243,7 @@
 
 def own_kernel(
     span, halo, doc_far, far_info_ref, q_ref, g_ref, k_ref, v_ref,
-    low_ref, high_ref, gw_low_ref, gw_high_ref, stat_ref, mask_ref, tail_ref, out_far, dq_far, dk_far, dv_far,
+    low_ref, high_ref, gw_low_ref, gw_high_ref, stat_ref, mask_ref, qt_ref, gt_ref, tail_ref, out_far, dq_far, dk_far, dv_far,
     doc_ref, info_ref, row_ref, out_ref, dq_ref, dk_ref, dv_ref, doc_sem, sems,
 ):
     half = span // 2
@@ -295,6 +295,8 @@
         stat_ref[0:1, wide] = top
         stat_ref[1:2, wide] = jnp.concatenate([total[:, :half], total_high], axis=1)
         stat_ref[2:3, wide] = jnp.concatenate([inner[:, :half], inner_high], axis=1)
+    qt_ref[...] = side_by_side(q_ref).T
+    gt_ref[...] = side_by_side(g_ref).T
     gw_low_ref[...] = gw_low
     gw_high_ref[...] = gw_high
 
@@ -310,7 +312,7 @@
 
 
 def halo_kernel(
-    span, mask_ref, pair_ref, ring_ref, q_ref, g_ref, stat_ref, edge_ref, p_ref, ds_ref, row_ref, back_ref
+    span, mask_ref, pair_ref, ring_ref, q_ref, g_ref, qt_ref, gt_ref, stat_ref, edge_ref, p_ref, ds_ref, row_ref, back_ref
 ):
     queries = side_by_side(q_ref)
     grads = side_by_side(g_ref)
@@ -318,8 +320,8 @@
     device = device_index()
     edge = jnp.where((device % 2 == 1) | (device == ring_cut(1)), pair_ref[...], ring_ref[...])
     edge_ref[...] = edge
-    scores = dot(edge[:, :HD], queries, ROWS_BY_ROWS) * LOG2_SCALE + mask
-    grad_weights = dot(edge[:, HD:], grads, ROWS_BY_ROWS)
+    scores = dot(edge[:, :HD], qt_ref[...], PLAIN) * LOG2_SCALE + mask
+    grad_weights = dot(edge[:, HD:], gt_ref[...], PLAIN)
     own_top = stat_ref[0:1]
     top = jnp.maximum(jnp.max(scores, axis=0, keepdims=True), own_top)
     weights = jnp.exp2(scores - top)
@@ -328,9 +330,8 @@
     inner = stat_ref[2:3] * shift + jnp.sum(weights * grad_weights, axis=0, keepdims=True)
     share = 1.0 / total
     delta = inner * share
-    p = weights * share
-    p_low = p.astype(jnp.bfloat16)
-    ds_low = (p * (grad_weights - delta) * SCALE).astype(jnp.bfloat16)
+    p_low = (weights * share).astype(jnp.bfloat16)
+    ds_low = (weights * (share * SCALE) * (grad_weights - delta)).astype(jnp.bfloat16)
     back_ref[:, :HD] = dot(ds_low, queries, PLAIN).astype(back_ref.dtype)
     back_ref[:, HD:] = dot(p_low, grads, PLAIN).astype(back_ref.dtype)
     p_ref[...] = p_low
@@ -473,10 +474,10 @@
     )(key_rows, value_rows)
     edges = passed_on(last_rows, pair_rows, 1)
     inputs = (queries, out_grad, key_rows, value_rows)
-    low, high, gw_low, gw_high, stats, mask, tail, outputs, query_grad, key_grad, value_grad = pl.pallas_call(
+    low, high, gw_low, gw_high, stats, mask, near_qt, near_gt, tail, outputs, query_grad, key_grad, value_grad = pl.pallas_call(
         lambda *refs: own_kernel(span, halo, *refs),
         in_specs=[hbm] + [vmem] * 5,
-        out_specs=[vmem] * 7 + [hbm] * 4,
+        out_specs=[vmem] * 9 + [hbm] * 4,
         out_shape=[
             pltpu.VMEM((span // 2, GROUP * span), f32),
             pltpu.VMEM((span // 2, GROUP * span // 2), f32),
@@ -484,6 +485,8 @@
             pltpu.VMEM((span // 2, GROUP * span // 2), f32),
             pltpu.VMEM((8, GROUP * span), f32),
             pltpu.VMEM((halo, span), f32),
+            pltpu.VMEM((HD, GROUP * span), bf16),
+            pltpu.VMEM((HD, GROUP * span), bf16),
             pltpu.VMEM((halo, 2 * HD), f32),
         ]
         + results_far,
@@ -499,7 +502,7 @@
     )(*far(doc_start), *near(info), *inputs)
     edge, p_edge, ds_edge, rows, back = pl.pallas_call(
         lambda *refs: halo_kernel(span, *refs),
-        in_specs=[vmem] * 6,
+        in_specs=[vmem] * 8,
         out_specs=[vmem] * 5,
         out_shape=[
             pltpu.VMEM((halo, 2 * HD), bf16),
@@ -510,7 +513,7 @@
         ],
         compiler_params=params,
         name="halo_grads",
-    )(*near(mask, *edges), *inputs[:2], *near(stats))
+    )(*near(mask, *edges), *inputs[:2], *near(near_qt, near_gt, stats))
     returned = passed_on(back, back, -1)
     outputs, query_grad, key_grad, value_grad, tail = pl.pallas_call(
         lambda *refs: rest_kernel(span, halo, *refs),

time: 10.7 us -> 10.7 us (level)
  no operation moved by 1% of the time
where the time goes in v2:
time: 10.7 us; the launch traced here: 10.5 us
  Pallas kernels  4.34 us (41%)
  waiting for transfers between devices  3.23 us (30%)
  starting transfers between devices  2.18 us (20%)
  between operations  0.73 us (7%)
    ppermute x2, waiting for transfers between devices, passed_on(): return (by_pair, lax.ppermute(value, ('seq', 'head'), rings))  2.99 us
    ppermute x2, starting transfers between devices, passed_on(): return (by_pair, lax.ppermute(value, ('seq', 'head'), rings))  2.06 us
    pallas_call x1, Pallas kernels, span_on_device(): pl.pallas_call(lambda *refs: rest_kernel(span, halo, *refs), in_specs=[vm...  1.65 us
    pallas_call x1, Pallas kernels, span_on_device(): pl.pallas_call(lambda *refs: pack_kernel(span, halo, *refs), in_specs=[hb...  0.86 us
    pallas_call x1, Pallas kernels, span_on_device(): pl.pallas_call(lambda *refs: own_kernel(span, halo, *refs), in_specs=[hbm...  0.69 us
    pallas_call x1, Pallas kernels, span_on_device(): pl.pallas_call(lambda *refs: tail_kernel(span, halo, *refs), in_specs=[vm...  0.64 us
    pallas_call x1, Pallas kernels, span_on_device(): pl.pallas_call(lambda *refs: halo_kernel(span, *refs), in_specs=[vmem] *...  0.49 us
    ppermute x2, waiting for transfers between devices, passed_on(): by_pair = lax.ppermute(pair_value, ('seq', 'head'), pairs)  0.24 us
  transfers between devices with their start and end apart: 4, of which 3 were waited for; matrix products, arithmetic and copies ran while one was open for 0% of the time, Pallas kernels for 22%

profile of v2, /device:TPU:7, one launch (start us, length us, event | category | flops | bytes accessed | tf_op | source)
XLA Modules:
  0.0 10.5 jit_solution(3733803779354669194)
XLA Ops:
  0.6 0.0 copy-start.3
  0.6 0.0 copy-start.2
  0.7 0.0 copy-start
  0.7 0.0 copy-start.1
  0.7 0.9 %pack.1 = (bf16[64,256]{1,0:T(8,128)(2,1)S(1)}, s32[8,128]{1,0:T(8,128)S(1)}) custom-call(s32[32]{0:T(128)} %refs_0_.5, bf16[256,128]{1,0:T(8,128)(2,1)} %refs_2_.5, bf16[256,128]{1,0:T(8,128)(2,1)} %refs_3_.5), custom_call_target="tpu_custom_call" | custom-call | flops 4000000000 | bytes 4194304 | tf_op jit(solution)/shard_map/pack/pallas_call | solution.py:457
  1.5 1.0 %collective-permute-start.1 = (bf16[64,256]{1,0:T(8,128)(2,1)S(1)}, bf16[64,256]{1,0:T(8,128)(2,1)S(1)}, u32[]{:S(2)}, u32[]{:S(2)}) collective-permute-start(bf16[64,256]{1,0:T(8,128)(2,1)S(1)} %get-tuple-element.33), channel_id=1, source_target_pairs={{0,1},{1,2},{2,3},{3,4},{4,5},{5,6},{6,7},{7,8},{8,9},{9,10},{10,1... | collective-permute-start | bytes 98312 | tf_op jit(solution)/shard_map/ppermute | solution.py:441
  2.6 0.0 copy-done.3
  2.6 0.0 copy-done.2
  2.6 0.0 collective-permute-start
  2.6 0.0 copy-done
  2.6 0.0 copy-done.1
  2.6 0.7 %own_scores.1 = (f32[128,1024]{1,0:T(8,128)S(1)}, f32[128,512]{1,0:T(8,128)S(1)}, f32[128,1024]{1,0:T(8,128)S(1)}, f32[128,512]{1,0:T(8,128)S(1)}, f32[8,1024]{1...) custom-call(s32[32]{0:T(128)} %refs_0_.5, ...), custom_call_target="tpu_custom_call" | custom-call | tf_op jit(solution)/shard_map/own_scores/pallas_call | solution.py:477
  3.3 0.2 %collective-permute-done.1.refs_2_ = bf16[64,256]{1,0:T(8,128)(2,1)S(1)} collective-permute-done((bf16[64,256]{1,0:T(8,128)(2,1)S(1)}, bf16[64,256]{1,0:T(8,128)(2,1)S(1)}, u32[]{:S(2)}, u32[]{:S(2)}) %collective-permute-start.1) | collective-permute-done | bytes 32800 | tf_op jit(solution)/shard_map/ppermute | solution.py:441
  3.6 0.2 %collective-permute-done.refs_1_ = bf16[64,256]{1,0:T(8,128)(2,1)S(1)} collective-permute-done((bf16[64,256]{1,0:T(8,128)(2,1)S(1)}, bf16[64,256]{1,0:T(8,128)(2,1)S(1)}, u32[]{:S(2)}, u32[]{:S(2)}) %collective-permute-start) | collective-permute-done | bytes 32800 | tf_op jit(solution)/shard_map/ppermute | solution.py:440
  3.8 0.5 %halo_grads.1 = (bf16[64,256]{1,0:T(8,128)(2,1)S(1)}, bf16[64,1024]{1,0:T(8,128)(2,1)S(1)}, bf16[64,1024]{1,0:T(8,128)(2,1)S(1)}, f32[8,1024]{1,0:T(8,128)S(1)}, bf16[64,256]{1,0:T(8,128)(2,1)S(1)}) custom-call(f32[64,256]{1,0:T(8,128)S(1)} %get-tuple-element.32.refs_0_, bf16[64,256]{1,0:T(8,128)(2,1)S(1)} %collective-permute-done.refs_1_, ...), custom_call_target="tpu_custom_call" | custom-call | tf_op jit(solution)/shard_map/halo_grads/pallas_call | solution.py:503
  4.3 1.0 %collective-permute-start.3 = (bf16[64,256]{1,0:T(8,128)(2,1)S(1)}, bf16[64,256]{1,0:T(8,128)(2,1)S(1)}, u32[]{:S(2)}, u32[]{:S(2)}) collective-permute-start(bf16[64,256]{1,0:T(8,128)(2,1)S(1)} %get-tuple-element.53), channel_id=1, source_target_pairs={{1,0},{2,1},{3,2},{4,3},{5,4},{6,5},{7,6},{8,7},{9,8},{10,9},{11,1... | collective-permute-start | bytes 98312 | tf_op jit(solution)/shard_map/ppermute | solution.py:441
  5.4 0.1 collective-permute-start.2
  5.4 1.6 %own_grads.1 = (bf16[256,512]{1,0:T(8,128)(2,1)}, bf16[256,512]{1,0:T(8,128)(2,1)}, bf16[256,128]{1,0:T(8,128)(2,1)}, bf16[256,128]{1,0:T(8,128)(2,1)}, f32[64,256]{1,0:T(8,128)S(1)}) custom-call(bf16[256,512]{1,0:T(8,128)(2,1)S(1)} %copy-done, ...), custom_call_target="tpu_custom_call", output_to_operand_aliasing={{0}: (12, {}), {1}: (13, {}), {2}: (14, {}), {3}: (15, {}),... | custom-call | tf_op jit(solution)/shard_map/own_grads/pallas_call | solution.py:518
  7.1 2.8 %collective-permute-done.3.refs_2_ = bf16[64,256]{1,0:T(8,128)(2,1)S(1)} collective-permute-done((bf16[64,256]{1,0:T(8,128)(2,1)S(1)}, bf16[64,256]{1,0:T(8,128)(2,1)S(1)}, u32[]{:S(2)}, u32[]{:S(2)}) %collective-permute-start.3) | collective-permute-done | bytes 32800 | tf_op jit(solution)/shard_map/ppermute | solution.py:441
  9.8 0.0 collective-permute-done.2.refs_1_
  9.9 0.6 %tail_grads.1 = (bf16[256,128]{1,0:T(8,128)(2,1)}, bf16[256,128]{1,0:T(8,128)(2,1)}) custom-call(f32[64,256]{1,0:T(8,128)S(1)} %get-tuple-element.52.refs_0_, bf16[64,256]{1,0:T(8,128)(2,1)S(1)} %collective-permute-done.2.refs_1_, bf16[64,256]{1,0:T(8,128)(2,1)S(1)} %collective-permute-done.3.refs_2_, ...), custom_call_target="tpu_custom_call", output_to_operand_aliasing={{0}: (3, {}), {1}: (4, {})} | custom-call | tf_op jit(solution)/shard_map/tail_grads/pallas_call | solution.py:533
  (1 shorter events, 0.0 us)
Async XLA Ops:
  0.6 1.9 %copy-start.3 = (bf16[256,128]{1,0:T(8,128)(2,1)S(1)}, bf16[256,128]{1,0:T(8,128)(2,1)}, u32[]{:S(2)}) copy-start(bf16[256,128]{1,0:T(8,128)(2,1)} %refs_3_.5) | copy-start | bytes 196612
  0.6 1.9 %copy-start.2 = (bf16[256,128]{1,0:T(8,128)(2,1)S(1)}, bf16[256,128]{1,0:T(8,128)(2,1)}, u32[]{:S(2)}) copy-start(bf16[256,128]{1,0:T(8,128)(2,1)} %refs_2_.5) | copy-start | bytes 196612
  0.7 2.0 %copy-start = (bf16[256,512]{1,0:T(8,128)(2,1)S(1)}, bf16[256,512]{1,0:T(8,128)(2,1)}, u32[]{:S(2)}) copy-start(bf16[256,512]{1,0:T(8,128)(2,1)} %refs_0_.7) | copy-start | bytes 786436
  0.7 2.0 %copy-start.1 = (bf16[256,512]{1,0:T(8,128)(2,1)S(1)}, bf16[256,512]{1,0:T(8,128)(2,1)}, u32[]{:S(2)}) copy-start(bf16[256,512]{1,0:T(8,128)(2,1)} %refs_1_.5) | copy-start | bytes 786436
  1.5 2.0 %collective-permute-start.1 = (bf16[64,256]{1,0:T(8,128)(2,1)S(1)}, bf16[64,256]{1,0:T(8,128)(2,1)S(1)}, u32[]{:S(2)}, u32[]{:S(2)}) collective-permute-start(bf16[64,256]{1,0:T(8,128)(2,1)S(1)} %get-tuple-element.33), channel_id=1, source_target_pairs={{0,1},{1,2},{2,3},{3,4},{4,5},{5,6},{6,7},{7,8},{8,9},{9,10},{10,1... | collective-permute-start | bytes 98312 | tf_op jit(solution)/shard_map/ppermute | solution.py:441
  2.6 1.2 %collective-permute-start = (bf16[64,256]{1,0:T(8,128)(2,1)S(1)}, bf16[64,256]{1,0:T(8,128)(2,1)S(1)}, u32[]{:S(2)}, u32[]{:S(2)}) collective-permute-start(bf16[64,256]{1,0:T(8,128)(2,1)S(1)} %pair_pack.1), channel_id=1, source_target_pairs={{0,1},{1,0},{2,3},{3,2},{4,5},{5,4},{6,7},{7,6},{8,9},{9,8},{10,11... | collective-permute-start | bytes 98312 | tf_op jit(solution)/shard_map/ppermute | solution.py:440
  4.3 5.5 %collective-permute-start.3 = (bf16[64,256]{1,0:T(8,128)(2,1)S(1)}, bf16[64,256]{1,0:T(8,128)(2,1)S(1)}, u32[]{:S(2)}, u32[]{:S(2)}) collective-permute-start(bf16[64,256]{1,0:T(8,128)(2,1)S(1)} %get-tuple-element.53), channel_id=1, source_target_pairs={{1,0},{2,1},{3,2},{4,3},{5,4},{6,5},{7,6},{8,7},{9,8},{10,9},{11,1... | collective-permute-start | bytes 98312 | tf_op jit(solution)/shard_map/ppermute | solution.py:441
  5.4 4.5 %collective-permute-start.2 = (bf16[64,256]{1,0:T(8,128)(2,1)S(1)}, bf16[64,256]{1,0:T(8,128)(2,1)S(1)}, u32[]{:S(2)}, u32[]{:S(2)}) collective-permute-start(bf16[64,256]{1,0:T(8,128)(2,1)S(1)} %get-tuple-element.53), channel_id=1, source_target_pairs={{1,0},{0,1},{3,2},{2,3},{5,4},{4,5},{7,6},{6,7},{9,8},{8,9},{11,10... | collective-permute-start | bytes 98312 | tf_op jit(solution)/shard_map/ppermute | solution.py:440
